TPU v7x, 32 devices: a whole 2x2x4 slice. The times are simulated.
32 devices in a mesh: sub: 4 (over z), grp: 8 (over y, x, core).
Axes of the slice: x: 2, y: 2, z: 4, core: 2. Of those that a mesh axis runs over, the one named last changes fastest.
Arguments:
- schur: bfloat16 [128, 1024, 1024], P(('sub', 'grp')), as said below
- mortar: bfloat16 [128, 8, 128, 128], P(('sub', 'grp')), may hold values from -0.5 to 0.5
- partner: int32 [128, 4], P(('sub', 'grp')), may hold values from 0 to 15, as said below
- corner_map: int32 [128, 8], P(('sub', 'grp')), may hold values from 0 to 127
- coarse_inv: float32 [4, 128, 128], P('sub'), as said below
- load: float32 [128, 1024, 384], P(('sub', 'grp')), may hold values from -6 to 6
Outputs:
- solution: float32 [128, 1024, 384], P(('sub', 'grp'))
Inputs may be any that keep to these rules, and one draw needn't show every extreme that they name: `partner`: within the 4 subdomains of one device, the entries form a permutation of 0 to 15. `schur`: each matrix is symmetric positive definite. `coarse_inv`: each matrix is symmetric positive definite.
All inputs are finite; a program needn't handle non-finite values.
Results may differ from a plain program's by a relative error of at most 0.0025.
Values may be sent and summed in bfloat16 or wider, within the bound.
No kernel may reach another device: no remote copies, remote signals or barrier semaphores. Data moves between devices by JAX's collectives and lax.ppermute only.
A program may use at most 128 MiB of HBM per device.

v0:
```python
import jax
import jax.numpy as jnp
from jax import lax
from jax.sharding import PartitionSpec as P

ITERS = 2


def shifted(block, axis, distance):
    devices = range(lax.axis_size(axis))
    route = [((i - distance) % len(devices), i) for i in devices]
    return lax.ppermute(block, axis, route)


def face_terms(direction, schur, mortar, partner):
    subdoms = direction.shape[0]
    order = direction.shape[1]
    columns = direction.shape[2]
    faces_all = mortar.shape[1]
    block = mortar.shape[2]
    half_faces = faces_all // 2
    dir_half = direction.astype(jnp.bfloat16)
    stiff = jnp.einsum("sij,sjr->sir", schur, dir_half, preferred_element_type=jnp.float32)
    face_rows = dir_half.reshape(subdoms, faces_all, block, columns)
    traces = jnp.einsum(
        "sfij,sfjr->sfir", mortar, face_rows, preferred_element_type=jnp.float32
    ).astype(jnp.bfloat16)
    upper = traces[:, :half_faces].reshape(subdoms * half_faces, block, columns)
    lower = traces[:, half_faces:].reshape(subdoms * half_faces, block, columns)
    mates = partner.reshape(-1)
    inverse = jnp.argsort(mates)
    reordered = jnp.take(upper, inverse, axis=0)
    lower_mate = shifted(reordered, "sub", 1)
    jump_lower = (lower.astype(jnp.float32) - lower_mate.astype(jnp.float32)).astype(jnp.bfloat16)
    above = shifted(lower, "sub", -1)
    upper_mate = jnp.take(above, mates, axis=0)
    jump_upper = (upper.astype(jnp.float32) - upper_mate.astype(jnp.float32)).astype(jnp.bfloat16)
    jump_all = jnp.concatenate(
        [
            jump_upper.reshape(subdoms, half_faces, block, columns),
            jump_lower.reshape(subdoms, half_faces, block, columns),
        ],
        axis=1,
    )
    pulled = jnp.einsum("sfji,sfjr->sfir", mortar, jump_all, preferred_element_type=jnp.float32)
    return stiff + pulled.reshape(subdoms, order, columns)


def squares(residual):
    return lax.psum(jnp.sum(residual * residual, axis=(0, 1)), ("sub", "grp"))


def on_device(schur, mortar, partner, corner_map, coarse_inv, load):
    order = load.shape[1]
    corner_count = corner_map.shape[1]
    coarse_count = coarse_inv.shape[1]
    stride = order // corner_count
    onehot = (corner_map[..., None] == jnp.arange(coarse_count, dtype=jnp.int32)).astype(
        jnp.float32
    )
    coarse_matrix = coarse_inv[0]
    solution = jnp.zeros_like(load)
    residual = load
    direction = load
    norm_now = squares(residual)
    for step in range(ITERS):
        partial_value = face_terms(direction, schur, mortar, partner)
        corners = direction[:, ::stride, :]
        local_sum = jnp.einsum("sco,scr->or", onehot, corners, precision=lax.Precision.HIGHEST)
        local_dot = jnp.sum(direction * partial_value, axis=(0, 1))
        coarse_sum = lax.psum(local_sum.astype(jnp.bfloat16), "grp").astype(jnp.float32)
        group_dot = lax.psum(local_dot.astype(jnp.bfloat16), "grp").astype(jnp.float32)
        coarse_val = jnp.dot(coarse_matrix, coarse_sum, precision=lax.Precision.HIGHEST)
        corner_add = jnp.einsum("sco,or->scr", onehot, coarse_val, precision=lax.Precision.HIGHEST)
        image = partial_value.at[:, ::stride, :].add(corner_add)
        curvature = lax.psum(group_dot + jnp.sum(coarse_sum * coarse_val, axis=0), "sub")
        image, curvature = (image, curvature)
        step_len = norm_now / curvature
        solution = solution + step_len * direction
        if step + 1 < ITERS:
            residual = residual - step_len * image
            norm_next = squares(residual)
            direction = residual + norm_next / norm_now * direction
            norm_now = norm_next
    return solution


def solution(mesh):
    return jax.shard_map(
        on_device,
        mesh=mesh,
        in_specs=(
            P(("sub", "grp"), None, None),
            P(("sub", "grp"), None, None, None),
            P(("sub", "grp"), None),
            P(("sub", "grp"), None),
            P("sub", None, None),
            P(("sub", "grp"), None, None),
        ),
        out_specs=P(("sub", "grp"), None, None),
        check_vma=False,
    )
```

profile of v0, /device:TPU:0, one launch (start us, length us, event | category | flops | bytes accessed | tf_op | source)
XLA Modules:
  0.0 398.2 jit_solution(7781319759656753900)
XLA Ops:
  6.5 3.2 convert_element_type.76
  9.8 1.0 convolution_convert_fusion
  10.8 1.5 fusion.33
  12.3 5.1 %collective-permute-start = (bf16[16,128,384]{2,1,0:T(8,128)(2,1)}, bf16[16,128,384]{2,1,0:T(8,128)(2,1)}, u32[]{:S(2)}, u32[]{:S(2)}) collective-permute-start(bf16[16,128,384]{2,1,0:T(8,128)(2,1)} %bitcast.2), channel_id=1, source_target_pairs={{8,0},{16,8},{24,16},{0,24},{9,1},{17,9},{25,17},{1,25},{10,2},{18... | collective-permute-start | bytes 4718600 | tf_op jit(solution)/shard_map/ppermute | solution.py:12
  17.5 1.2 sort.19
  18.8 1.9 gather_fusion.1
  20.7 2.8 broadcast_select_fusion.1
  23.5 2.8 slice.20
  26.3 1.0 fusion.17
  27.4 6.6 %copy.8 = f32[4,1024,384]{1,2,0:T(8,128)} copy(f32[4,1024,384]{2,1,0:T(8,128)} %param.13) | data formatting | bytes 12582912 | tf_op args[5]
  34.0 46.9 %all-reduce.3.cloned.1.call-done = bf16[128,384]{1,0:T(8,128)(2,1)} async-done(((bf16[128,384]{1,0:T(8,128)(2,1)}), bf16[128,384]{1,0:T(8,128)(2,1)}) %all-reduce.3.cloned.1.call-update) | async-done | bytes 98320 | tf_op jit(solution)/shard_map/psum | solution.py:71
  81.0 1.2 fusion.21
  82.4 3.3 gather_fusion
  85.8 2.1 subtract_convert_fusion.3
  87.9 2.5 subtract_convert_fusion.2
  90.4 3.7 fusion.5
  94.1 12.9 %multiply_reduce_fusion.1 = (bf16[384]{0:T(512)(128)(2,1)S(1)}, f32[384]{0:T(512)S(1)}, f32[4,1024,384]{2,1,0:T(8,128)}) fusion(f32[4,1024,384]{2,1,0:T(8,128)S(1)} %bitcast.79, f32[4,8,384,128]{2,3,1,0:T(8,128)} %fusion.5, bf16[4,1024,1024]{2,1,0:T(8,128)(2,1)} %param.8), kind=kOutput, calls=%fused_computation.13 | convolution fusion | flops 3230661632 | bytes 27265280 | tf_op jit(solution)/shard_map/sij,sjr->sir/dot_general | solution.py:23
  107.0 12.8 %psum.57 = bf16[384]{0:T(512)(128)(2,1)S(1)} all-reduce(bf16[384]{0:T(512)(128)(2,1)S(1)} %get-tuple-element.8), channel_id=1, replica_groups=mesh['sub'=4,'grp'=8] {'grp'}, use_global_device_ids=true, to_apply=%region_4.6 | all-reduce | flops 384 | bytes 1536 | tf_op jit(solution)/shard_map/psum | solution.py:72
  119.8 11.7 %psum.59 = f32[384]{0:T(512)S(1)} all-reduce(f32[384]{0:T(512)S(1)} %convert_add_fusion.1), channel_id=1, replica_groups=mesh['sub'=4,'grp'=8] {'sub'}, use_global_device_ids=true, to_apply=%region_7.9 | all-reduce | flops 384 | bytes 3072 | tf_op jit(solution)/shard_map/psum | solution.py:76
  131.5 37.0 %psum.56 = f32[384]{0:T(512)S(1)} all-reduce(f32[384]{0:T(512)S(1)} %get-tuple-element.9), channel_id=1, replica_groups=mesh['sub'=4,'grp'=8] {'sub','grp'}, use_global_device_ids=true, to_apply=%region_1.0 | all-reduce | flops 384 | bytes 3072 | tf_op jit(solution)/shard_map/psum | solution.py:50
  168.5 9.5 %copy.10 = f32[4,1024,384]{2,0,1:T(4,128)} copy(f32[4,1024,384]{2,1,0:T(8,128)} %get-tuple-element.16) | data formatting | bytes 12582912 | tf_op jit(solution)/shard_map/add | solution.py:46
  178.0 2.1 scatter_fusion
  180.0 7.6 %copy.12 = f32[4,1024,384]{1,2,0:T(8,128)} copy(f32[4,1024,384]{2,0,1:T(4,128)} %scatter_fusion) | data formatting | bytes 12582912 | tf_op jit(solution)/shard_map/scatter-add | solution.py:75
  187.7 5.6 %multiply_reduce_fusion = f32[384]{0:T(512)S(1)} fusion(f32[4,1024,384]{1,2,0:T(8,128)} %copy.8, f32[4,1024,384]{1,2,0:T(8,128)} %copy.12, f32[384]{0:T(512)S(1)} %div.9), kind=kLoop, calls=%fused_computation.11 | loop fusion | flops 6291072 | bytes 12585984 | tf_op jit(solution)/shard_map/reduce_sum | solution.py:50
  193.3 42.2 %psum.60 = f32[384]{0:T(512)S(1)} all-reduce(f32[384]{0:T(512)S(1)} %multiply_reduce_fusion), channel_id=1, replica_groups=mesh['sub'=4,'grp'=8] {'sub','grp'}, use_global_device_ids=true, to_apply=%region_10.12 | all-reduce | flops 384 | bytes 3072 | tf_op jit(solution)/shard_map/psum | solution.py:50
  235.5 7.7 %convert_bitcast_fusion.1 = (bf16[4,48,8,8,128]{4,3,2,1,0:T(8,128)(2,1)S(1)}, f32[4,1024,384]{1,2,0:T(8,128)}) fusion(f32[4,1024,384]{1,2,0:T(8,128)} %copy.8, f32[384]{0:T(512)S(1)} %div.10, f32[4,1024,384]{1,2,0:T(8,128)} %copy.12, f32[384]{0:T(512)S(1)} %div.9), kind=kLoop, calls=%fused_computation.32 | loop fusion | flops 7864320 | bytes 22023168
  243.2 1.0 convert_bitcast_fusion
  244.2 1.4 fusion.32
  245.6 1.6 collective-permute-start.2
  247.1 1.9 gather_fusion.3
  249.0 2.8 broadcast_select_fusion
  252.3 4.3 %slice.23 = f32[4,8,384]{1,2,0:T(8,128)S(1)} slice(f32[4,1024,384]{1,2,0:T(8,128)} %get-tuple-element.11), slice={[0:4:1], [0:1024:128], [0:384:1]} | slice | bytes 98304 | tf_op jit(solution)/shard_map/slice | solution.py:68
  256.6 1.2 fusion.18
  257.9 53.1 %all-reduce.5.cloned.1.call-done = bf16[128,384]{1,0:T(8,128)(2,1)} async-done(((bf16[128,384]{1,0:T(8,128)(2,1)}), bf16[128,384]{1,0:T(8,128)(2,1)}) %all-reduce.5.cloned.1.call-update) | async-done | bytes 98320 | tf_op jit(solution)/shard_map/psum | solution.py:71
  310.9 1.2 fusion.19
  312.1 2.8 collective-permute-done.2
  314.9 3.3 gather_fusion.2
  318.3 3.2 subtract_convert_fusion.1
  321.4 1.9 copy.16
  323.3 3.4 subtract_convert_fusion
  326.8 2.6 copy.17
  329.3 5.1 %fusion.9 = f32[4,8,384,128]{2,3,1,0:T(8,128)} fusion(bf16[4,8,128,128]{3,2,1,0:T(8,128)(2,1)S(1)} %copy-done, bf16[4,4,128,384]{3,2,1,0:T(8,128)(2,1)} %bitcast.87, bf16[4,4,128,384]{3,2,1,0:T(8,128)(2,1)S(1)} %bitcast.85), kind=kOutput, calls=%fused_computation.22 | convolution fusion | flops 404226048 | bytes 10485760 | tf_op jit(solution)/shard_map/sfji,sfjr->sfir/dot_general | solution.py:45
  334.4 6.5 %copy.27 = f32[4,1024,384]{1,2,0:T(8,128)} copy(f32[4,1024,384]{2,1,0:T(8,128)} %bitcast.80) | data formatting | bytes 12582912 | tf_op jit(solution)/shard_map/reshape | solution.py:46
  340.9 12.5 %fusion.1 = bf16[384]{0:T(512)(128)(2,1)S(1)} fusion(f32[4,1024,384]{1,2,0:T(8,128)} %get-tuple-element.11, f32[4,1024,384]{1,2,0:T(8,128)} %copy.27, bf16[4,1024,1024]{2,1,0:T(8,128)(2,1)} %param.8), kind=kOutput, calls=%fused_computation.8 | convolution fusion | flops 3227516416 | bytes 20972288 | tf_op jit(solution)/shard_map/sij,sjr->sir/dot_general | solution.py:23
  353.5 11.8 %psum.61 = bf16[384]{0:T(512)(128)(2,1)S(1)} all-reduce(bf16[384]{0:T(512)(128)(2,1)S(1)} %fusion.1), channel_id=1, replica_groups=mesh['sub'=4,'grp'=8] {'grp'}, use_global_device_ids=true, to_apply=%region_12.14 | all-reduce | flops 384 | bytes 1536 | tf_op jit(solution)/shard_map/psum | solution.py:72
  365.3 9.9 %psum.63 = f32[384]{0:T(512)S(1)} all-reduce(f32[384]{0:T(512)S(1)} %convert_add_fusion), channel_id=1, replica_groups=mesh['sub'=4,'grp'=8] {'sub'}, use_global_device_ids=true, to_apply=%region_15.17 | all-reduce | flops 384 | bytes 3072 | tf_op jit(solution)/shard_map/psum | solution.py:76
  375.2 9.6 %multiply_add_fusion = f32[4,1024,384]{1,2,0:T(8,128)} fusion(f32[4,1024,384]{1,2,0:T(8,128)} %get-tuple-element.11, f32[4,1024,384]{1,2,0:T(8,128)} %copy.8, f32[384]{0:T(512)S(1)} %div.11, f32[384]{0:T(512)S(1)} %div.9), kind=kLoop, calls=%fused_computation.9 | loop fusion | flops 4718592 | bytes 18877440 | tf_op jit(solution)/shard_map/add | solution.py:79
  384.8 6.6 %copy.21 = f32[4,1024,384]{2,1,0:T(8,128)} copy(f32[4,1024,384]{1,2,0:T(8,128)} %multiply_add_fusion) | data formatting | bytes 12582912 | tf_op jit(solution)/shard_map/add | solution.py:79
  (38 shorter events, 1.0 us)
Async XLA Ops:
  6.5 3.2 copy-start
  6.5 74.4 %all-reduce.3.cloned.1.call-start = ((), (), s32[]{:S(2)}) async-start(), calls=%async_computation | async-start | bytes 196608 | tf_op jit(solution)/shard_map/psum | solution.py:71
  10.8 6.6 %copy-start.3 = (s32[4,4]{1,0:T(4,128)S(1)}, s32[4,4]{1,0:T(4,128)}, u32[]{:S(2)}) copy-start(s32[4,4]{1,0:T(4,128)} %param.10) | copy-start | bytes 196
  12.3 70.1 %collective-permute-start = (bf16[16,128,384]{2,1,0:T(8,128)(2,1)}, bf16[16,128,384]{2,1,0:T(8,128)(2,1)}, u32[]{:S(2)}, u32[]{:S(2)}) collective-permute-start(bf16[16,128,384]{2,1,0:T(8,128)(2,1)} %bitcast.2), channel_id=1, source_target_pairs={{8,0},{16,8},{24,16},{0,24},{9,1},{17,9},{25,17},{1,25},{10,2},{18... | collective-permute-start | bytes 4718600 | tf_op jit(solution)/shard_map/ppermute | solution.py:12
  18.8 7.5 %copy-start.2 = (s32[4,8]{1,0:T(4,128)S(1)}, s32[4,8]{1,0:T(4,128)}, u32[]{:S(2)}) copy-start(s32[4,8]{1,0:T(4,128)} %param.11) | copy-start | bytes 388
  23.5 64.4 %collective-permute-start.1 = (bf16[16,128,384]{2,1,0:T(8,128)(2,1)}, bf16[16,128,384]{2,1,0:T(8,128)(2,1)}, u32[]{:S(2)}, u32[]{:S(2)}) collective-permute-start(bf16[16,128,384]{2,1,0:T(8,128)(2,1)} %broadcast_select_fusion.1), channel_id=1, source_target_pairs={{24,0},{0,8},{8,16},{16,24},{25,1},{1,9},{9,17},{17,25},{26,2},{2,... | collective-permute-start | bytes 4718600 | tf_op jit(solution)/shard_map/ppermute | solution.py:12
  27.3 283.6 %all-reduce.5.cloned.1.call-start = ((), (), s32[]{:S(2)}) async-start(), calls=%async_computation.1 | async-start | bytes 196608 | tf_op jit(solution)/shard_map/psum | solution.py:71
  27.4 53.5 %copy-start.1 = (f32[1,128,128]{2,1,0:T(8,128)S(1)}, f32[1,128,128]{2,1,0:T(8,128)}, u32[]{:S(2)}) copy-start(f32[1,128,128]{2,1,0:T(8,128)} %param.12) | copy-start | bytes 196612
  87.9 6.2 %slice-start = ((s8[6291456]{0:T(1024)(128)(4,1)}), s8[4194304]{0:T(1024)(128)(4,1)S(1)}, s32[]{:S(2)}) async-start(s8[6291456]{0:T(1024)(128)(4,1)} %bitcast.78), calls=%async_computation.2 | async-start | bytes 8388608
  90.4 3.7 slice-start.1
  245.6 69.3 %collective-permute-start.2 = (bf16[16,128,384]{1,2,0:T(8,128)(2,1)}, bf16[16,128,384]{1,2,0:T(8,128)(2,1)}, u32[]{:S(2)}, u32[]{:S(2)}) collective-permute-start(bf16[16,128,384]{1,2,0:T(8,128)(2,1)} %bitcast.16), channel_id=1, source_target_pairs={{8,0},{16,8},{24,16},{0,24},{9,1},{17,9},{25,17},{1,25},{10,2},{18... | collective-permute-start | bytes 4718600 | tf_op jit(solution)/shard_map/ppermute | solution.py:12
  251.8 71.5 %collective-permute-start.3 = (bf16[16,128,384]{1,2,0:T(8,128)(2,1)}, bf16[16,128,384]{1,2,0:T(8,128)(2,1)}, u32[]{:S(2)}, u32[]{:S(2)}) collective-permute-start(bf16[16,128,384]{1,2,0:T(8,128)(2,1)} %broadcast_select_fusion), channel_id=1, source_target_pairs={{24,0},{0,8},{8,16},{16,24},{25,1},{1,9},{9,17},{17,25},{26,2},{2,... | collective-permute-start | bytes 4718600 | tf_op jit(solution)/shard_map/ppermute | solution.py:12
Sparse Core Ops, SparseCore 0:
  27.4 53.4 all-reduce.2
  258.0 52.8 all-reduce.4
where the time goes:
time: 399 us; the launch traced here: 398 us
  blocking collectives  125 us (31%)
  waiting for transfers between devices  103 us (26%)
  local copies, waits for them, and re-layouts  61.9 us (16%)
  other arithmetic  46.2 us (12%)
  matrix products  41.1 us (10%)
  between operations  13.6 us (3%)
  starting transfers between devices  7.15 us (2%)
    psum x2, waiting for transfers between devices, on_device(): lax.psum(local_sum.astype(jnp.bfloat16), 'grp').astype(jnp.float32)  100 us
    psum x2, blocking collectives, squares(): return lax.psum(jnp.sum(residual * residual, axis=(0, 1)), ('sub', 'grp'))  79.2 us
    dot_general x2, matrix products, face_terms(): jnp.einsum('sij,sjr->sir', schur, dir_half, preferred_element_type=jnp.fl...  25.4 us
    psum x2, blocking collectives, on_device(): lax.psum(local_dot.astype(jnp.bfloat16), 'grp').astype(jnp.float32)  24.6 us
    psum x2, blocking collectives, on_device(): lax.psum(group_dot + jnp.sum(coarse_sum * coarse_val, axis=0), 'sub')  21.6 us
    add x1, other arithmetic, on_device(): solution = solution + step_len * direction  9.61 us
    add x1, local copies, waits for them, and re-layouts, face_terms(): return stiff + pulled.reshape(subdoms, order, columns)  9.48 us
    dot_general x2, matrix products, face_terms(): jnp.einsum('sfji,sfjr->sfir', mortar, jump_all, preferred_element_type=jn...  8.78 us
  transfers between devices with their start and end apart: 6, of which 3 were waited for; matrix products, arithmetic and copies ran while one was open for 11% of the time, Pallas kernels for 0%

commit v1 on v0

--- a/solution.py
+++ b/solution.py
@@ -47,7 +47,7 @@
 
 
 def squares(residual):
-    return lax.psum(jnp.sum(residual * residual, axis=(0, 1)), ("sub", "grp"))
+    return lax.psum(lax.psum(jnp.sum(residual * residual, axis=(0, 1)), "grp"), "sub")
 
 
 def on_device(schur, mortar, partner, corner_map, coarse_inv, load):

time: 399 us -> 352 us (0.88)
  blocking collectives: 125 us -> 81 us
    psum x2 -> x4, blocking collectives: 79.2 us -> 43.8 us  [the longest x2 23.8 us: squares(): lax.psum(jnp.sum(residual * residual, axis=(0, 1)), 'grp')]
    psum x2 -> x1, blocking collectives: 21.6 us -> 11.7 us  [on_device(): lax.psum(group_dot + jnp.sum(coarse_sum * coarse_val, axis=0), 'sub')]
  transfers between devices with their start and end apart: 6 -> 6, of which waited for: 3 -> 2; matrix products, arithmetic and copies ran while one was open for 11% -> 12% of each run, Pallas kernels for 0% -> 0%
where the time goes in v1:
time: 352 us; the launch traced here: 351 us
  waiting for transfers between devices  99.6 us (28%)
  blocking collectives  81 us (23%)
  local copies, waits for them, and re-layouts  61.9 us (18%)
  other arithmetic  46.2 us (13%)
  matrix products  41.1 us (12%)
  between operations  13.6 us (4%)
  starting transfers between devices  7.15 us (2%)
    psum x2, waiting for transfers between devices, on_device(): lax.psum(local_sum.astype(jnp.bfloat16), 'grp').astype(jnp.float32)  99.5 us
    psum x2, blocking collectives, on_device(): lax.psum(local_dot.astype(jnp.bfloat16), 'grp').astype(jnp.float32)  25.6 us
    dot_general x2, matrix products, face_terms(): jnp.einsum('sij,sjr->sir', schur, dir_half, preferred_element_type=jnp.fl...  25.4 us
    psum x2, blocking collectives, squares(): lax.psum(jnp.sum(residual * residual, axis=(0, 1)), 'grp')  23.8 us
    psum x2, blocking collectives, squares(): lax.psum(lax.psum(jnp.sum(residual * residual, axis=(0, 1)), 'grp'), 'sub')  20 us
    psum x1, blocking collectives, on_device(): lax.psum(group_dot + jnp.sum(coarse_sum * coarse_val, axis=0), 'sub')  11.7 us
    add x1, other arithmetic, on_device(): solution = solution + step_len * direction  9.61 us
    add x1, local copies, waits for them, and re-layouts, face_terms(): return stiff + pulled.reshape(subdoms, order, columns)  9.48 us
  transfers between devices with their start and end apart: 6, of which 2 were waited for; matrix products, arithmetic and copies ran while one was open for 12% of the time, Pallas kernels for 0%

profile of v1, /device:TPU:0, one launch (start us, length us, event | category | flops | bytes accessed | tf_op | source)
XLA Modules:
  0.0 350.6 jit_solution(14547406304257943895)
XLA Ops:
  6.5 3.2 convert_element_type.76
  9.8 1.0 convolution_convert_fusion
  10.8 1.5 fusion.33
  12.3 5.1 %collective-permute-start = (bf16[16,128,384]{2,1,0:T(8,128)(2,1)}, bf16[16,128,384]{2,1,0:T(8,128)(2,1)}, u32[]{:S(2)}, u32[]{:S(2)}) collective-permute-start(bf16[16,128,384]{2,1,0:T(8,128)(2,1)} %bitcast.2), channel_id=1, source_target_pairs={{8,0},{16,8},{24,16},{0,24},{9,1},{17,9},{25,17},{1,25},{10,2},{18... | collective-permute-start | bytes 4718600 | tf_op jit(solution)/shard_map/ppermute | solution.py:12
  17.5 1.2 sort.19
  18.8 1.9 gather_fusion.1
  20.7 2.8 broadcast_select_fusion.1
  23.5 2.8 slice.20
  26.3 1.0 fusion.17
  27.4 6.6 %copy.8 = f32[4,1024,384]{1,2,0:T(8,128)} copy(f32[4,1024,384]{2,1,0:T(8,128)} %param.13) | data formatting | bytes 12582912 | tf_op args[5]
  34.0 46.9 %all-reduce.4.cloned.1.call-done = bf16[128,384]{1,0:T(8,128)(2,1)} async-done(((bf16[128,384]{1,0:T(8,128)(2,1)}), bf16[128,384]{1,0:T(8,128)(2,1)}) %all-reduce.4.cloned.1.call-update) | async-done | bytes 98320 | tf_op jit(solution)/shard_map/psum | solution.py:71
  81.0 1.2 fusion.21
  82.4 3.3 gather_fusion
  85.8 2.1 subtract_convert_fusion.3
  87.9 2.5 subtract_convert_fusion.2
  90.4 3.7 %fusion.5 = f32[4,8,384,128]{2,3,1,0:T(8,128)} fusion(bf16[4,8,128,128]{3,2,1,0:T(8,128)(2,1)S(1)} %copy-done, bf16[4,4,128,384]{3,2,1,0:T(8,128)(2,1)S(1)} %bitcast.86, bf16[4,4,128,384]{3,2,1,0:T(8,128)(2,1)S(1)} %bitcast.84), kind=kOutput, calls=%fused_computation.18 | convolution fusion | flops 404226048 | bytes 10485760 | tf_op jit(solution)/shard_map/sfji,sfjr->sfir/dot_general | solution.py:45
  94.1 12.9 %multiply_reduce_fusion.1 = (bf16[384]{0:T(512)(128)(2,1)S(1)}, f32[384]{0:T(512)S(1)}, f32[4,1024,384]{2,1,0:T(8,128)}) fusion(f32[4,1024,384]{2,1,0:T(8,128)S(1)} %bitcast.79, f32[4,8,384,128]{2,3,1,0:T(8,128)} %fusion.5, bf16[4,1024,1024]{2,1,0:T(8,128)(2,1)} %param.8), kind=kOutput, calls=%fused_computation.13 | convolution fusion | flops 3230661632 | bytes 27265280 | tf_op jit(solution)/shard_map/sij,sjr->sir/dot_general | solution.py:23
  107.0 12.8 %psum.72 = bf16[384]{0:T(512)(128)(2,1)S(1)} all-reduce(bf16[384]{0:T(512)(128)(2,1)S(1)} %get-tuple-element.8), channel_id=1, replica_groups=mesh['sub'=4,'grp'=8] {'grp'}, use_global_device_ids=true, to_apply=%region_5.7 | all-reduce | flops 384 | bytes 1536 | tf_op jit(solution)/shard_map/psum | solution.py:72
  119.8 12.0 %psum.70 = f32[384]{0:T(512)S(1)} all-reduce(f32[384]{0:T(512)S(1)} %get-tuple-element.9), channel_id=1, replica_groups=mesh['sub'=4,'grp'=8] {'grp'}, use_global_device_ids=true, to_apply=%region_1.0 | all-reduce | flops 384 | bytes 3072 | tf_op jit(solution)/shard_map/psum | solution.py:50
  131.8 9.5 %copy.10 = f32[4,1024,384]{2,0,1:T(4,128)} copy(f32[4,1024,384]{2,1,0:T(8,128)} %get-tuple-element.18) | data formatting | bytes 12582912 | tf_op jit(solution)/shard_map/add | solution.py:46
  141.2 2.1 scatter_fusion
  143.3 7.6 %copy.12 = f32[4,1024,384]{1,2,0:T(8,128)} copy(f32[4,1024,384]{2,0,1:T(4,128)} %scatter_fusion) | data formatting | bytes 12582912 | tf_op jit(solution)/shard_map/scatter-add | solution.py:75
  151.0 11.7 %all-reduce = (f32[384]{0:T(512)S(1)}, f32[384]{0:T(512)S(1)}) all-reduce(f32[384]{0:T(512)S(1)} %psum.70, f32[384]{0:T(512)S(1)} %convert_add_fusion.1), channel_id=1, replica_groups=mesh['sub'=4,'grp'=8] {'sub'}, use_global_device_ids=true, to_apply=%region_2.0 | all-reduce | flops 768 | bytes 6144 | tf_op jit(solution)/shard_map/psum | solution.py:50
  162.6 5.6 %multiply_reduce_fusion = f32[384]{0:T(512)S(1)} fusion(f32[4,1024,384]{1,2,0:T(8,128)} %copy.8, f32[4,1024,384]{1,2,0:T(8,128)} %copy.12, f32[384]{0:T(512)S(1)} %div.9), kind=kLoop, calls=%fused_computation.11 | loop fusion | flops 6291072 | bytes 12585984 | tf_op jit(solution)/shard_map/reduce_sum | solution.py:50
  168.2 11.8 %psum.75 = f32[384]{0:T(512)S(1)} all-reduce(f32[384]{0:T(512)S(1)} %multiply_reduce_fusion), channel_id=1, replica_groups=mesh['sub'=4,'grp'=8] {'grp'}, use_global_device_ids=true, to_apply=%region_11.13 | all-reduce | flops 384 | bytes 3072 | tf_op jit(solution)/shard_map/psum | solution.py:50
  180.0 8.4 %psum.76 = f32[384]{0:T(512)S(1)} all-reduce(f32[384]{0:T(512)S(1)} %psum.75), channel_id=1, replica_groups=mesh['sub'=4,'grp'=8] {'sub'}, use_global_device_ids=true, to_apply=%region_12.14 | all-reduce | flops 384 | bytes 3072 | tf_op jit(solution)/shard_map/psum | solution.py:50
  188.4 7.7 %convert_bitcast_fusion.1 = (bf16[4,48,8,8,128]{4,3,2,1,0:T(8,128)(2,1)S(1)}, f32[4,1024,384]{1,2,0:T(8,128)}) fusion(f32[4,1024,384]{1,2,0:T(8,128)} %copy.8, f32[384]{0:T(512)S(1)} %div.10, f32[4,1024,384]{1,2,0:T(8,128)} %copy.12, f32[384]{0:T(512)S(1)} %div.9), kind=kLoop, calls=%fused_computation.32 | loop fusion | flops 7864320 | bytes 22023168
  196.0 1.0 convert_bitcast_fusion
  197.0 1.4 fusion.32
  198.5 2.0 collective-permute-start.2
  200.5 1.9 gather_fusion.3
  202.4 2.8 broadcast_select_fusion
  205.2 4.3 %slice.23 = f32[4,8,384]{1,2,0:T(8,128)S(1)} slice(f32[4,1024,384]{1,2,0:T(8,128)} %get-tuple-element.13), slice={[0:4:1], [0:1024:128], [0:384:1]} | slice | bytes 98304 | tf_op jit(solution)/shard_map/slice | solution.py:68
  209.5 1.2 fusion.18
  210.8 52.6 %all-reduce.6.cloned.1.call-done = bf16[128,384]{1,0:T(8,128)(2,1)} async-done(((bf16[128,384]{1,0:T(8,128)(2,1)}), bf16[128,384]{1,0:T(8,128)(2,1)}) %all-reduce.6.cloned.1.call-update) | async-done | bytes 98320 | tf_op jit(solution)/shard_map/psum | solution.py:71
  263.4 1.2 fusion.19
  264.6 3.3 gather_fusion.2
  267.9 3.2 subtract_convert_fusion.1
  271.1 1.9 copy.16
  273.0 3.4 subtract_convert_fusion
  276.4 2.6 copy.17
  279.0 5.1 %fusion.9 = f32[4,8,384,128]{2,3,1,0:T(8,128)} fusion(bf16[4,8,128,128]{3,2,1,0:T(8,128)(2,1)S(1)} %copy-done, bf16[4,4,128,384]{3,2,1,0:T(8,128)(2,1)} %bitcast.87, bf16[4,4,128,384]{3,2,1,0:T(8,128)(2,1)S(1)} %bitcast.85), kind=kOutput, calls=%fused_computation.22 | convolution fusion | flops 404226048 | bytes 10485760 | tf_op jit(solution)/shard_map/sfji,sfjr->sfir/dot_general | solution.py:45
  284.1 6.5 %copy.27 = f32[4,1024,384]{1,2,0:T(8,128)} copy(f32[4,1024,384]{2,1,0:T(8,128)} %bitcast.80) | data formatting | bytes 12582912 | tf_op jit(solution)/shard_map/reshape | solution.py:46
  290.6 12.5 %fusion.1 = bf16[384]{0:T(512)(128)(2,1)S(1)} fusion(f32[4,1024,384]{1,2,0:T(8,128)} %get-tuple-element.13, f32[4,1024,384]{1,2,0:T(8,128)} %copy.27, bf16[4,1024,1024]{2,1,0:T(8,128)(2,1)} %param.8), kind=kOutput, calls=%fused_computation.8 | convolution fusion | flops 3227516416 | bytes 20972288 | tf_op jit(solution)/shard_map/sij,sjr->sir/dot_general | solution.py:23
  303.1 12.8 %psum.77 = bf16[384]{0:T(512)(128)(2,1)S(1)} all-reduce(bf16[384]{0:T(512)(128)(2,1)S(1)} %fusion.1), channel_id=1, replica_groups=mesh['sub'=4,'grp'=8] {'grp'}, use_global_device_ids=true, to_apply=%region_14.16 | all-reduce | flops 384 | bytes 1536 | tf_op jit(solution)/shard_map/psum | solution.py:72
  315.9 11.7 %psum.79 = f32[384]{0:T(512)S(1)} all-reduce(f32[384]{0:T(512)S(1)} %convert_add_fusion), channel_id=1, replica_groups=mesh['sub'=4,'grp'=8] {'sub'}, use_global_device_ids=true, to_apply=%region_17.19 | all-reduce | flops 384 | bytes 3072 | tf_op jit(solution)/shard_map/psum | solution.py:76
  327.6 9.6 %multiply_add_fusion = f32[4,1024,384]{1,2,0:T(8,128)} fusion(f32[4,1024,384]{1,2,0:T(8,128)} %get-tuple-element.13, f32[4,1024,384]{1,2,0:T(8,128)} %copy.8, f32[384]{0:T(512)S(1)} %div.11, f32[384]{0:T(512)S(1)} %div.9), kind=kLoop, calls=%fused_computation.9 | loop fusion | flops 4718592 | bytes 18877440 | tf_op jit(solution)/shard_map/add | solution.py:79
  337.2 6.6 %copy.21 = f32[4,1024,384]{2,1,0:T(8,128)} copy(f32[4,1024,384]{1,2,0:T(8,128)} %multiply_add_fusion) | data formatting | bytes 12582912 | tf_op jit(solution)/shard_map/add | solution.py:79
  (39 shorter events, 0.5 us)
Async XLA Ops:
  6.5 3.2 copy-start
  6.5 74.4 %all-reduce.4.cloned.1.call-start = ((), (), s32[]{:S(2)}) async-start(), calls=%async_computation | async-start | bytes 196608 | tf_op jit(solution)/shard_map/psum | solution.py:71
  10.8 6.6 %copy-start.3 = (s32[4,4]{1,0:T(4,128)S(1)}, s32[4,4]{1,0:T(4,128)}, u32[]{:S(2)}) copy-start(s32[4,4]{1,0:T(4,128)} %param.10) | copy-start | bytes 196
  12.3 70.1 %collective-permute-start = (bf16[16,128,384]{2,1,0:T(8,128)(2,1)}, bf16[16,128,384]{2,1,0:T(8,128)(2,1)}, u32[]{:S(2)}, u32[]{:S(2)}) collective-permute-start(bf16[16,128,384]{2,1,0:T(8,128)(2,1)} %bitcast.2), channel_id=1, source_target_pairs={{8,0},{16,8},{24,16},{0,24},{9,1},{17,9},{25,17},{1,25},{10,2},{18... | collective-permute-start | bytes 4718600 | tf_op jit(solution)/shard_map/ppermute | solution.py:12
  18.8 7.5 %copy-start.2 = (s32[4,8]{1,0:T(4,128)S(1)}, s32[4,8]{1,0:T(4,128)}, u32[]{:S(2)}) copy-start(s32[4,8]{1,0:T(4,128)} %param.11) | copy-start | bytes 388
  23.5 64.4 %collective-permute-start.1 = (bf16[16,128,384]{2,1,0:T(8,128)(2,1)}, bf16[16,128,384]{2,1,0:T(8,128)(2,1)}, u32[]{:S(2)}, u32[]{:S(2)}) collective-permute-start(bf16[16,128,384]{2,1,0:T(8,128)(2,1)} %broadcast_select_fusion.1), channel_id=1, source_target_pairs={{24,0},{0,8},{8,16},{16,24},{25,1},{1,9},{9,17},{17,25},{26,2},{2,... | collective-permute-start | bytes 4718600 | tf_op jit(solution)/shard_map/ppermute | solution.py:12
  27.3 236.1 %all-reduce.6.cloned.1.call-start = ((), (), s32[]{:S(2)}) async-start(), calls=%async_computation.1 | async-start | bytes 196608 | tf_op jit(solution)/shard_map/psum | solution.py:71
  27.4 53.5 %copy-start.1 = (f32[1,128,128]{2,1,0:T(8,128)S(1)}, f32[1,128,128]{2,1,0:T(8,128)}, u32[]{:S(2)}) copy-start(f32[1,128,128]{2,1,0:T(8,128)} %param.12) | copy-start | bytes 196612
  87.9 6.2 %slice-start = ((s8[6291456]{0:T(1024)(128)(4,1)}), s8[4194304]{0:T(1024)(128)(4,1)S(1)}, s32[]{:S(2)}) async-start(s8[6291456]{0:T(1024)(128)(4,1)} %bitcast.78), calls=%async_computation.2 | async-start | bytes 8388608
  90.4 3.7 %slice-start.1 = ((s8[6291456]{0:T(1024)(128)(4,1)}), s8[2097152]{0:T(1024)(128)(4,1)S(1)}, s32[]{:S(2)}) async-start(s8[6291456]{0:T(1024)(128)(4,1)} %bitcast.78), calls=%async_computation.3 | async-start | bytes 4194304
  198.5 66.1 %collective-permute-start.2 = (bf16[16,128,384]{1,2,0:T(8,128)(2,1)}, bf16[16,128,384]{1,2,0:T(8,128)(2,1)}, u32[]{:S(2)}, u32[]{:S(2)}) collective-permute-start(bf16[16,128,384]{1,2,0:T(8,128)(2,1)} %bitcast.16), channel_id=1, source_target_pairs={{8,0},{16,8},{24,16},{0,24},{9,1},{17,9},{25,17},{1,25},{10,2},{18... | collective-permute-start | bytes 4718600 | tf_op jit(solution)/shard_map/ppermute | solution.py:12
  205.2 67.8 %collective-permute-start.3 = (bf16[16,128,384]{1,2,0:T(8,128)(2,1)}, bf16[16,128,384]{1,2,0:T(8,128)(2,1)}, u32[]{:S(2)}, u32[]{:S(2)}) collective-permute-start(bf16[16,128,384]{1,2,0:T(8,128)(2,1)} %broadcast_select_fusion), channel_id=1, source_target_pairs={{24,0},{0,8},{8,16},{16,24},{25,1},{1,9},{9,17},{17,25},{26,2},{2,... | collective-permute-start | bytes 4718600 | tf_op jit(solution)/shard_map/ppermute | solution.py:12
Sparse Core Ops, SparseCore 0:
  27.4 53.4 all-reduce.3
  210.9 52.4 all-reduce.5
